TPU v7x, 32 devices: a whole 2x2x4 slice. The times are simulated.
32 devices in a mesh: groups: 2 (over x), ctx: 16 (over z, y, core).
Axes of the slice: x: 2, y: 2, z: 4, core: 2. Of those that a mesh axis runs over, the one named last changes fastest.
Arguments:
- inputs: bfloat16 [4096, 8192], P(None, ('groups', 'ctx')), parts along dimension 1, may hold values from -4 to 4
- projections: bfloat16 [512, 8192], P(None, ('groups', 'ctx')), parts along dimension 1, may hold values from -7 to 7
- step_sizes: bfloat16 [64, 8192], P(None, ('groups', 'ctx')), parts along dimension 1, may hold values from 0.0019989014 to 0.019897461
- log_rates: float32 [64], replicated, may hold values from -12 to 3
- skip_gain: float32 [64], replicated, may hold values from 0.5 to 1.5
- packing: int32 [32, 256], P(('groups', 'ctx')), parts along dimension 0, may hold values from 0 to 255, as said below
- prompt_sizes: int32 [8], P('groups'), parts along dimension 0, may hold values from 1 to 3072, 4096 in all
Outputs:
- ssd_output: bfloat16 [4096, 8192], P(None, ('groups', 'ctx')), parts along dimension 1
There are 2 independent parts, one for each index of `groups`. A program takes and returns all parts, laid end to end along the dimension named above; an argument that names none is the same for every part. Nothing has to cross between parts.
Inputs may be any that keep to these rules, and one draw needn't show every extreme that they name: `packing`: each row names every one of the loader's 256 tokens once. `prompt_sizes`: the lengths add up to 4096.
All inputs are finite; a program needn't handle non-finite values.
Results may differ from a plain program's by a relative error of at most 0.001.
The roundings to bfloat16 on the way count: a program that leaves them out, or rounds other values in their place, can miss the bound.
Values may be sent and summed in bfloat16 or wider, within the bound.
A program may use at most 320 MiB of HBM per device.

v0:
```python
import jax
import jax.numpy as jnp
from jax import lax
from jax.sharding import PartitionSpec as P

G = 4
BLOCK = 128


def carried_in(value, axis, join, neutral):
    count, mine = (lax.axis_size(axis), lax.axis_index(axis))
    pieces = jax.tree.map(lambda part: lax.all_gather(part, axis), value)
    so_far = jax.tree.map(
        lambda part, zero: jnp.full_like(part, 0) + jnp.asarray(zero, part.dtype), value, neutral
    )

    def lap(position, so_far):
        longer = join(so_far, jax.tree.map(lambda part: part[position], pieces))
        return jax.tree.map(lambda new, old: jnp.where(position < mine, new, old), longer, so_far)

    return lax.fori_loop(0, count - 1, lap, so_far)


def block_setup(block_dt, resets, decay_rate):
    step_size = block_dt.astype(jnp.float32)
    log_decay = jnp.cumsum(step_size * decay_rate[:, None], axis=1)
    before_reset = jnp.cumsum(resets) == 0
    return (step_size, log_decay, before_reset)


def block_state(block_x, block_bc, segment, setup):
    step_size, log_decay, before_reset = setup
    head_count = log_decay.shape[0]
    length = block_x.shape[1]
    per_group = head_count // G
    x_heads = block_x.reshape(G, per_group, -1, length)
    maps = block_bc.reshape(G, 2, -1, length)
    last_decay = log_decay[:, -1:]
    into_end = (
        jnp.where((segment == segment[-1])[None, :], jnp.exp(last_decay - log_decay), 0.0)
        * step_size
    )
    weighted = (x_heads * into_end.reshape(G, per_group, 1, length)).astype(jnp.bfloat16)
    block_total = jnp.einsum(
        "ghpj,gnj->ghpn", weighted, maps[:, 0], preferred_element_type=jnp.float32
    )
    block_keep = jnp.where(before_reset[-1], jnp.exp(last_decay[:, 0]), 0.0)
    return (block_keep, block_total.reshape(head_count, x_heads.shape[2], maps.shape[2]))


def block_output(block_x, block_bc, segment, setup, skip_gain, carry_in):
    step_size, log_decay, before_reset = setup
    head_count = log_decay.shape[0]
    length = block_x.shape[1]
    per_group = head_count // G
    head_width = block_x.shape[0] // head_count
    states = block_bc.shape[0] // (2 * G)
    column_index = jnp.arange(length, dtype=jnp.int32)
    allowed = (column_index[:, None] >= column_index[None, :]) & (
        segment[:, None] == segment[None, :]
    )

    def group_part(operands):
        x_group, map_group, step_group, decay_group, carry_group, skip_group = operands
        x_heads = x_group.reshape(per_group, head_width, length)
        input_map = map_group[0]
        output_map = map_group[1]
        decay_gap = decay_group[:, :, None] - decay_group[:, None, :]
        decay_mask = jnp.exp(jnp.where(allowed[None], decay_gap, -jnp.inf))
        inner_gram = jnp.einsum(
            "ni,nj->ij", output_map, input_map, preferred_element_type=jnp.float32
        )
        mixing = (inner_gram[None] * (decay_mask * step_group[:, None, :])).astype(jnp.bfloat16)
        within = jnp.einsum("hij,hpj->hpi", mixing, x_heads, preferred_element_type=jnp.float32)
        opened = jnp.where(before_reset[None, :], jnp.exp(decay_group), 0.0)
        carried = jnp.einsum(
            "hpn,ni->hpi",
            carry_group.astype(jnp.bfloat16),
            output_map,
            preferred_element_type=jnp.float32,
        )
        result = (
            within
            + carried * opened[:, None, :]
            + skip_group[:, None, None] * x_heads.astype(jnp.float32)
        )
        return result.reshape(-1, length).astype(jnp.bfloat16)

    grouped = (
        block_x.reshape(G, -1, length),
        block_bc.reshape(G, 2, states, length),
        step_size.reshape(G, per_group, length),
        log_decay.reshape(G, per_group, length),
        carry_in.reshape(G, per_group, head_width, states),
        skip_gain.reshape(G, per_group),
    )
    outputs = lax.map(group_part, grouped)
    return outputs.reshape(-1, length)


def combine(earlier, later):
    return (earlier[0] * later[0], later[0][:, None, None] * earlier[1] + later[1])


def per_device(inputs, projections, step_sizes, log_rates, skip_gain, packing, prompt_sizes):
    own_rows = inputs.shape[1]
    head_count = log_rates.shape[0]
    states = projections.shape[0] // (2 * G)
    head_width = inputs.shape[0] // head_count
    send_order = packing[0]
    owned_x, owned_bc, owned_dt = (
        lax.all_to_all(
            jnp.take(inputs, send_order, axis=1), "ctx", split_axis=1, concat_axis=1, tiled=True
        ),
        lax.all_to_all(
            jnp.take(projections, send_order, axis=1),
            "ctx",
            split_axis=1,
            concat_axis=1,
            tiled=True,
        ),
        lax.all_to_all(
            jnp.take(step_sizes, send_order, axis=1), "ctx", split_axis=1, concat_axis=1, tiled=True
        ),
    )
    position = lax.axis_index("ctx") * own_rows + jnp.arange(own_rows, dtype=jnp.int32)
    prompt_start = jnp.cumsum(prompt_sizes) - prompt_sizes
    segment = jnp.sum((position[:, None] >= prompt_start[None, :]).astype(jnp.int32), axis=1) - 1
    resets = jnp.sum((position[:, None] == prompt_start[None, :]).astype(jnp.int32), axis=1)
    decay_rate = -jnp.exp(log_rates)
    block_count = own_rows // BLOCK
    setups = []
    keeps = []
    totals = []
    dev_keep = jnp.ones((head_count,), jnp.float32)
    dev_total = jnp.zeros((head_count, head_width, states), jnp.float32)
    for block_id in range(block_count):
        lower = block_id * BLOCK
        upper = lower + BLOCK
        setup = block_setup(owned_dt[:, lower:upper], resets[lower:upper], decay_rate)
        block_keep, block_total = block_state(
            owned_x[:, lower:upper], owned_bc[:, lower:upper], segment[lower:upper], setup
        )
        setups.append(setup)
        keeps.append(block_keep)
        totals.append(block_total)
        dev_total = block_keep[:, None, None] * dev_total + block_total
        dev_keep = dev_keep * block_keep
    identity = (
        jnp.ones((head_count,), jnp.float32),
        jnp.zeros((head_count, head_width, states), jnp.float32),
    )
    carry_in = carried_in((dev_keep, dev_total), "ctx", combine, identity)[1]
    results = []
    for block_id in range(block_count):
        lower = block_id * BLOCK
        upper = lower + BLOCK
        results.append(
            block_output(
                owned_x[:, lower:upper],
                owned_bc[:, lower:upper],
                segment[lower:upper],
                setups[block_id],
                skip_gain,
                carry_in,
            )
        )
        carry_in = keeps[block_id][:, None, None] * carry_in + totals[block_id]
    return jnp.concatenate(results, axis=1)


def solution(mesh):
    in_specs = (
        P(None, ("groups", "ctx")),
        P(None, ("groups", "ctx")),
        P(None, ("groups", "ctx")),
        P(),
        P(),
        P(("groups", "ctx"), None),
        P("groups"),
    )
    out_specs = P(None, ("groups", "ctx"))
    return jax.shard_map(
        per_device, mesh=mesh, in_specs=in_specs, out_specs=out_specs, check_vma=False
    )
```

profile of v0, /device:TPU:26, one launch (start us, length us, event | category | flops | bytes accessed | tf_op | source)
XLA Modules:
  0.0 352.2 jit_solution(8487469282059257848)
XLA Ops:
  11.7 6.1 %all-to-all-start.2 = ((bf16[16,2,512]{2,1,0:T(2,128)(2,1)}), bf16[16,2,512]{2,1,0:T(2,128)(2,1)S(1)}, u32[]{:S(2)}, u32[]{:S(2)}) async-start(bf16[16,2,512]{2,1,0:T(2,128)(2,1)} %reshape.453), calls=%async_computation.2 | async-start | bytes 65536 | tf_op jit(solution)/shard_map/all_to_all | solution.py:122
  20.8 2.9 copy.56
  23.8 3.2 gather_fusion
  26.9 6.0 %all-to-all-start.1 = ((bf16[512,16,16]{0,2,1:T(8,128)(2,1)}), bf16[512,16,16]{0,2,1:T(8,128)(2,1)S(1)}, u32[]{:S(2)}, u32[]{:S(2)}) async-start(bf16[512,16,16]{0,2,1:T(8,128)(2,1)} %broadcast_select_fusion.1), calls=%async_computation.1 | async-start | bytes 524288 | tf_op jit(solution)/shard_map/all_to_all | solution.py:115
  33.0 3.2 broadcast_select_fusion
  36.1 4.1 %all-to-all-done.1 = bf16[512,16,16]{0,2,1:T(8,128)(2,1)S(1)} async-done(((bf16[512,16,16]{0,2,1:T(8,128)(2,1)}), bf16[512,16,16]{0,2,1:T(8,128)(2,1)S(1)}, u32[]{:S(2)}, u32[]{:S(2)}) %all-to-all-start.1) | async-done | bytes 262176 | tf_op jit(solution)/shard_map/all_to_all | solution.py:115
  40.2 6.4 %all-to-all-start = ((bf16[4096,16,16]{0,2,1:T(8,128)(2,1)}), bf16[4096,16,16]{0,2,1:T(8,128)(2,1)S(1)}, u32[]{:S(2)}, u32[]{:S(2)}) async-start(bf16[4096,16,16]{0,2,1:T(8,128)(2,1)} %broadcast_select_fusion), calls=%async_computation | async-start | bytes 4194304 | tf_op jit(solution)/shard_map/all_to_all | solution.py:112
  57.2 32.8 %all-to-all-done = bf16[4096,16,16]{0,2,1:T(8,128)(2,1)S(1)} async-done(((bf16[4096,16,16]{0,2,1:T(8,128)(2,1)}), bf16[4096,16,16]{0,2,1:T(8,128)(2,1)S(1)}, u32[]{:S(2)}, u32[]{:S(2)}) %all-to-all-start) | async-done | bytes 2097184 | tf_op jit(solution)/shard_map/all_to_all | solution.py:112
  99.2 28.4 %all-reduce = f32[1024]{0:T(1024)S(1)} all-reduce(f32[1024]{0:T(1024)S(1)} %dynamic-update-slice), channel_id=2, replica_groups=mesh['groups'=2,'ctx'=16] {'ctx'}, use_global_device_ids=true, to_apply=%add | all-reduce | flops 1024 | bytes 8192
  128.9 140.0 %all-gather.3.cloned.1.call-done = f32[16,64,64,64]{3,2,1,0:T(8,128)} async-done(((f32[1,64,64,64]{3,2,1,0:T(8,128)}), f32[16,64,64,64]{3,2,1,0:T(8,128)}) %all-gather.3.cloned.1.call-update) | async-done | bytes 16777232 | tf_op jit(solution)/shard_map/all_gather | solution.py:12
  268.9 41.8 %while.38 = (s32[]{:T(128)}, f32[64,64,64]{2,1,0:T(8,128)S(1)}, s32[]{:T(128)}, f32[16,64]{1,0:T(8,128)}, f32[16,64,64,64]{3,2,1,0:T(8,128)}, /*index=5*/s32[]{:T(128)}, s32[]{:T(128)}) while((s32[]{:T(128)}, f32[64,64,64]{2,1,0:T(8,128)S(1)}, s32[]{:T(128)}, f32[16,64]{1,0:T(8,128)}, f32[16,64,64,64]{3,2,1,0:T(8,128)}, ...), condition=%wide.region_8.9_spmd.clone, body=%wide.region_7.8_spmd.clone.sunk | while | flops 1048580 | bytes 3146601 | solution.py:21
  269.6 2.1 fusion.105
  272.4 2.1 fusion.105
  278.0 2.1 fusion.105
  280.8 2.1 fusion.105
  286.3 2.1 fusion.105
  289.1 2.1 fusion.105
  291.9 2.1 fusion.105
  294.7 2.1 fusion.105
  300.3 2.1 fusion.105
  313.1 17.8 %while.36 = (s32[]{:T(128)}, bf16[4,1024,128]{2,1,0:T(8,128)(2,1)}, bf16[4,1024,128]{2,1,0:T(8,128)(2,1)}, bf16[4,2,64,128]{3,2,1,0:T(8,128)(2,1)S(1)}, f32[4,16...) while((s32[]{:T(128)}, bf16[4,1024,128]{2,1,0:T(8,128)(2,1)}, ...), condition=%wide.region_10.11_spmd.clone, body=%wide.region_9.10_spmd.clone.sunk | while | flops 54577152 | bytes 3428257 | solution.py:97
  330.9 2.9 bitcast_add_fusion.1
  334.0 8.7 %while.37 = (s32[]{:T(128)}, bf16[4,1024,128]{2,1,0:T(8,128)(2,1)S(1)}, bf16[4,1024,128]{2,1,0:T(8,128)(2,1)S(1)}, bf16[4,2,64,128]{3,2,1,0:T(8,128)(2,1)S(1)}, ...) while((s32[]{:T(128)}, ...), condition=%wide.region_12.13_spmd.clone, body=%wide.region_11.12_spmd.clone.sunk | while | flops 54577152 | bytes 3427749 | solution.py:97
  342.6 2.8 pad_maximum_fusion
  (188 shorter events, 79.8 us)
Async XLA Ops:
  11.7 15.2 %all-to-all-start.2 = ((bf16[16,2,512]{2,1,0:T(2,128)(2,1)}), bf16[16,2,512]{2,1,0:T(2,128)(2,1)S(1)}, u32[]{:S(2)}, u32[]{:S(2)}) async-start(bf16[16,2,512]{2,1,0:T(2,128)(2,1)} %reshape.453), calls=%async_computation.2 | async-start | bytes 65536 | tf_op jit(solution)/shard_map/all_to_all | solution.py:122
  26.9 13.3 %all-to-all-start.1 = ((bf16[512,16,16]{0,2,1:T(8,128)(2,1)}), bf16[512,16,16]{0,2,1:T(8,128)(2,1)S(1)}, u32[]{:S(2)}, u32[]{:S(2)}) async-start(bf16[512,16,16]{0,2,1:T(8,128)(2,1)} %broadcast_select_fusion.1), calls=%async_computation.1 | async-start | bytes 524288 | tf_op jit(solution)/shard_map/all_to_all | solution.py:115
  36.1 10.6 %copy-start.12 = (s32[4]{0:T(128)S(1)}, s32[4]{0:T(128)}, u32[]{:S(2)}) copy-start(s32[4]{0:T(128)} %param.19) | copy-start | bytes 52
  36.1 13.3 %copy-start.13 = (f32[64]{0:T(128)S(1)}, f32[64]{0:T(128)}, u32[]{:S(2)}) copy-start(f32[64]{0:T(128)} %param.16) | copy-start | bytes 772
  40.2 49.8 %all-to-all-start = ((bf16[4096,16,16]{0,2,1:T(8,128)(2,1)}), bf16[4096,16,16]{0,2,1:T(8,128)(2,1)S(1)}, u32[]{:S(2)}, u32[]{:S(2)}) async-start(bf16[4096,16,16]{0,2,1:T(8,128)(2,1)} %broadcast_select_fusion), calls=%async_computation | async-start | bytes 4194304 | tf_op jit(solution)/shard_map/all_to_all | solution.py:112
  46.6 222.3 %all-gather.3.cloned.1.call-start = ((), (), s32[]{:S(2)}) async-start(), calls=%async_computation.3 | async-start | bytes 35651584 | tf_op jit(solution)/shard_map/all_gather | solution.py:12
  48.8 0.7 copy-start.4
  91.1 1.2 copy-start.2
  91.8 1.7 copy-start.1
  93.0 0.8 copy-start.3
  93.4 1.3 copy-start
  93.4 1.3 copy-start.8
  93.4 1.3 copy-start.11
  96.4 0.7 copy-start.10
  96.4 1.3 copy-start.14
  96.4 2.5 copy-start.5
  96.4 2.5 copy-start.9
  310.7 2.4 copy-start.6
  313.1 17.8 %copy-start.7 = (f32[64]{0:T(128)S(1)}, f32[64]{0:T(128)}, u32[]{:S(2)}) copy-start(f32[64]{0:T(128)} %get-tuple-element.354) | copy-start | bytes 772
Sparse Core Ops, SparseCore 0:
  96.6 172.3 all-gather.2
where the time goes:
time: 356 us; the launch traced here: 352 us
  waiting for transfers between devices  177 us (50%)
  other arithmetic  54.9 us (15%)
  local copies, waits for them, and re-layouts  42.3 us (12%)
  blocking collectives  28.4 us (8%)
  starting transfers between devices  18.6 us (5%)
  matrix products  16 us (4%)
  between operations  14.3 us (4%)
    all_gather x1, waiting for transfers between devices, carried_in(): pieces = jax.tree.map(lambda part: lax.all_gather(part, axis), value)  140 us
    all_to_all x1, waiting for transfers between devices, per_device(): lax.all_to_all(jnp.take(inputs, send_order, axis=1), 'ctx', split_axis=1,...  32.8 us
    select_n x15, other arithmetic, lap(): jnp.where(position < mine, new, old)  31.1 us
    unnamed x1, blocking collectives  28.4 us
    unnamed x43, local copies, waits for them, and re-layouts  10.6 us
    mul x15, local copies, waits for them, and re-layouts, combine(): later[0][:, None, None] * earlier[1] + later[1]  10.4 us
    dot_general x8, matrix products, group_part(): jnp.einsum('hpn,ni->hpi', carry_group.astype(jnp.bfloat16), output_map, p...  9.38 us
  transfers between devices with their start and end apart: 4, of which 3 were waited for; matrix products, arithmetic and copies ran while one was open for 7% of the time, Pallas kernels for 0%

commit v1 on v0

v1 whole, which is shorter than its diff:
```python
import functools
import jax
import jax.numpy as jnp
from jax import lax
from jax.experimental import pallas as pl
from jax.experimental.pallas import tpu as pltpu
from jax.sharding import PartitionSpec as P

G = 4
BLOCK = 128
LANES = 128
PLANE = 4
VLIM = 60 * 1024 * 1024
F32 = jnp.float32
BF16 = jnp.bfloat16
MESH = pl.DeviceIdType.MESH


def dot_nt(a, b):
    return lax.dot_general(a, b, (((1,), (1,)), ((), ())), preferred_element_type=F32)


def prep_kernel(pack_ref, x_ref, bc_ref, dt_ref, y_ref, d_ref):
    tok = x_ref.shape[1]
    rows = lax.broadcasted_iota(jnp.int32, (tok, tok), 0)
    pick = jnp.where(rows == pack_ref[...], 1.0, 0.0).astype(F32)
    pick_t = pick.T.astype(BF16)
    wx = x_ref.shape[0]
    y_ref[:, :wx] = dot_nt(pick_t, x_ref[...]).astype(BF16)
    y_ref[:, wx:] = dot_nt(pick_t, bc_ref[...]).astype(BF16)

    @pl.when(pl.program_id(0) == 0)
    def _():
        dt = dot_nt(pick_t, dt_ref[...]).astype(BF16)
        d_ref[...] = jnp.concatenate(
            [dt, jnp.zeros((tok, d_ref.shape[1] - dt.shape[1]), BF16)], axis=1
        )


def exchange_kernel(n, y_ref, d_ref, yo_ref, do_ref, ssem, rsem, lsem):
    me = lax.axis_index("ctx")
    barrier = pltpu.get_barrier_semaphore()

    def greet(off, _):
        pl.semaphore_signal(
            barrier, inc=1, device_id={"ctx": lax.rem(me + off, n)}, device_id_type=MESH
        )
        return 0

    lax.fori_loop(1, n, greet, 0)
    own_y = pltpu.make_async_copy(y_ref.at[me], yo_ref.at[me], lsem.at[0])
    own_d = pltpu.make_async_copy(d_ref.at[me], do_ref.at[me], lsem.at[1])
    own_y.start()
    own_d.start()
    pl.semaphore_wait(barrier, n - 1)

    def copies(off):
        to = lax.rem(me + off, n)
        frm = me
        y = pltpu.make_async_remote_copy(
            y_ref.at[to], yo_ref.at[frm], ssem.at[0, off], rsem.at[0, off],
            device_id={"ctx": to}, device_id_type=MESH)
        d = pltpu.make_async_remote_copy(
            d_ref.at[to], do_ref.at[frm], ssem.at[1, off], rsem.at[1, off],
            device_id={"ctx": to}, device_id_type=MESH)
        return y, d

    half = n // 2

    def start_d(off, _):
        copies(off)[1].start()
        return 0

    def start_pair(i, _):
        copies(half - i)[0].start()

        @pl.when(i > 0)
        def _():
            copies(half + i)[0].start()

        return 0

    lax.fori_loop(1, n, start_d, 0)
    lax.fori_loop(0, half, start_pair, 0)

    def finish(off, _):
        y, d = copies(off)
        d.wait()
        y.wait()
        return 0

    lax.fori_loop(1, n, finish, 0)
    own_y.wait()
    own_d.wait()


def starts_of(sizes_ref):
    out = []
    at = jnp.int32(0)
    for s in range(sizes_ref.shape[0]):
        out.append(at)
        at = at + sizes_ref[s]
    return out


def segment_of(position, starts):
    seg = jnp.zeros(position.shape, jnp.int32)
    for at in starts:
        seg = seg + (position >= at).astype(jnp.int32)
    return seg


def decay_of(dt, rate):
    t = dt.shape[0]
    tri = jnp.where(
        lax.broadcasted_iota(jnp.int32, (t, t), 0) >= lax.broadcasted_iota(jnp.int32, (t, t), 1),
        1.0, 0.0).astype(F32)
    return jnp.dot(tri, dt * rate, preferred_element_type=F32, precision=lax.Precision.HIGHEST)


def spread(value, heads, width):
    rows = value.shape[0]
    per = LANES // width
    lane = lax.broadcasted_iota(jnp.int32, (rows, LANES), 1)
    out = []
    for q in range(heads // per):
        acc = jnp.broadcast_to(value[:, q * per:q * per + 1], (rows, LANES))
        for k in range(1, per):
            other = jnp.broadcast_to(value[:, q * per + k:q * per + k + 1], (rows, LANES))
            acc = jnp.where(lane >= k * width, other, acc)
        out.append(acc)
    return jnp.concatenate(out, axis=1)


def group_lanes(value, g, per_group):
    return pltpu.roll(value, lax.rem(LANES - g * per_group, LANES), 1)


def states_kernel(heads, width, states, sizes_ref, rate_ref, y_ref, d_ref, t_ref, t0_ref):
    g = pl.program_id(0)
    tok = y_ref.shape[0]
    wx = heads * width
    starts = starts_of(sizes_ref)
    base = lax.axis_index("ctx") * tok
    rate = group_lanes(-jnp.exp(rate_ref[...]), g, heads)[0:1]
    total = None
    for b in range(tok // BLOCK):
        lo = b * BLOCK
        first = base + lo
        last = first + BLOCK - 1
        dt = group_lanes(d_ref[lo:lo + BLOCK, :].astype(F32), g, heads)
        cum = decay_of(dt, rate)
        end = cum[BLOCK - 1:BLOCK, :]
        pos = first + lax.broadcasted_iota(jnp.int32, (BLOCK, LANES), 0)
        last_seg = jnp.int32(0)
        cut = jnp.int32(0)
        for at in starts:
            last_seg = last_seg + (last >= at).astype(jnp.int32)
            cut = cut + ((at >= first) & (at <= last)).astype(jnp.int32)
        same = segment_of(pos, starts) == last_seg
        into = jnp.where(same, jnp.exp(end - cum), 0.0) * dt
        weighted = (y_ref[lo:lo + BLOCK, :wx].astype(F32) * spread(into, heads, width)).astype(BF16)
        maps_t = y_ref[lo:lo + BLOCK, wx:].astype(F32).T
        in_map = maps_t[:states].astype(BF16)
        block_total = jnp.dot(in_map, weighted, preferred_element_type=F32)
        keep_h = jnp.where(cut == 0, jnp.exp(end), 0.0)
        keep = spread(jnp.broadcast_to(keep_h, (8, LANES)), heads, width)
        if total is None:
            total, gain = block_total, keep
        else:
            total = keep[0:1] * total + block_total
            gain = gain * keep
        if b < tok // BLOCK - 1:
            t0_ref[b, :states, :] = block_total
            t0_ref[b, states:, :] = keep
    t_ref[:states, :] = total
    t_ref[states:, :] = gain


def chain_kernel(n, states, chunks, t_ref, c_ref, early, first, chip, enter, leave, ssem, rsem):
    me = lax.axis_index("ctx")
    q = lax.rem(me, PLANE)
    z = me // PLANE
    nz = n // PLANE
    cw = t_ref.shape[1] // chunks
    barrier = pltpu.get_barrier_semaphore()

    def hail(to):
        pl.semaphore_signal(barrier, inc=1, device_id={"ctx": to}, device_id_type=MESH)

    @pl.when(q == 0)
    def _():
        hail(me + 1)
        pl.semaphore_wait(barrier, 1)

    @pl.when(q == 1)
    def _():
        hail(me - 1)
        hail(me + 2)
        pl.semaphore_wait(barrier, 2)

    @pl.when(q == 2)
    def _():
        hail(me + 1)
        pl.semaphore_wait(barrier, 1)

    @pl.when(q == 3)
    def _():
        hail(me - 1)
        hail(me - 2)

        @pl.when(z > 0)
        def _():
            hail(me - PLANE)

        @pl.when(z < nz - 1)
        def _():
            hail(me + PLANE)

        pl.semaphore_wait(barrier, 2 + jnp.where(z > 0, 1, 0) + jnp.where(z < nz - 1, 1, 0))

    def sl(ref, c):
        return ref.at[:, pl.ds(pl.multiple_of(c * cw, LANES), cw)]

    def push(kind, way, c, src, dst, to):
        return pltpu.make_async_remote_copy(
            sl(src, c), sl(dst, c), ssem.at[way, c], rsem.at[kind, c],
            device_id={"ctx": to}, device_id_type=MESH)

    EARLY, FIRST, ENTER = 0, 1, 2

    def lanes(c):
        return pl.ds(pl.multiple_of(c * cw, LANES), cw)

    def join(old, new):
        gain = new[states:states + 1]
        return jnp.concatenate([gain * old[:states] + new[:states], old[states:] * new[states:]], axis=0)

    def loop(body):
        def step(c, _):
            body(c)
            return 0
        lax.fori_loop(0, chunks, step, 0)

    @pl.when(q == 0)
    def _():
        loop(lambda c: push(EARLY, 0, c, t_ref, early, me + 1).start())

        def body(c):
            s = lanes(c)

            @pl.when(z > 0)
            def _():
                push(ENTER, 1, c, enter, enter, me + 1).wait_recv()
                c_ref[:, s] = enter[:, s]

            @pl.when(z == 0)
            def _():
                c_ref[:, s] = jnp.zeros((states, cw), F32)

        loop(body)
        loop(lambda c: push(EARLY, 0, c, t_ref, early, me + 1).wait_send())

    @pl.when(q == 1)
    def _():
        def up(c):
            s = lanes(c)
            push(EARLY, 0, c, t_ref, early, me - 1).wait_recv()
            chip[:, s] = join(early[:, s], t_ref[:, s])
            push(FIRST, 0, c, chip, first, me + 2).start()

        loop(up)

        def body(c):
            s = lanes(c)

            @pl.when(z > 0)
            def _():
                push(ENTER, 1, c, enter, enter, me - 1).wait_recv()
                push(ENTER, 1, c, enter, enter, me - 1).start()
                c_ref[:, s] = early[states:states + 1, s] * enter[:, s] + early[:states, s]

            @pl.when(z == 0)
            def _():
                c_ref[:, s] = early[:states, s]

        loop(body)
        loop(lambda c: push(FIRST, 0, c, chip, first, me + 2).wait_send())

        @pl.when(z > 0)
        def _():
            loop(lambda c: push(ENTER, 1, c, enter, enter, me - 1).wait_send())

    @pl.when(q == 2)
    def _():
        loop(lambda c: push(EARLY, 0, c, t_ref, early, me + 1).start())

        def body(c):
            s = lanes(c)
            push(FIRST, 1, c, first, first, me + 1).wait_recv()

            @pl.when(z > 0)
            def _():
                push(ENTER, 1, c, enter, enter, me + 1).wait_recv()
                c_ref[:, s] = first[states:states + 1, s] * enter[:, s] + first[:states, s]

            @pl.when(z == 0)
            def _():
                c_ref[:, s] = first[:states, s]

        loop(body)
        loop(lambda c: push(EARLY, 0, c, t_ref, early, me + 1).wait_send())

    @pl.when(q == 3)
    def _():
        def body(c):
            s = lanes(c)
            push(EARLY, 0, c, t_ref, early, me - 1).wait_recv()
            push(FIRST, 0, c, first, first, me - 1).wait_recv()
            push(FIRST, 0, c, first, first, me - 1).start()
            mine = join(first[:, s], early[:, s])
            whole = join(mine, t_ref[:, s])

            @pl.when(z > 0)
            def _():
                push(ENTER, 1, c, enter, enter, me - 1).wait_recv()
                came = enter[:, s]

                @pl.when(z < nz - 1)
                def _():
                    leave[:, s] = whole[states:states + 1] * came + whole[:states]
                    push(ENTER, 3, c, leave, enter, me + PLANE).start()

                push(ENTER, 2, c, enter, enter, me - 2).start()
                push(ENTER, 1, c, enter, enter, me - 1).start()
                c_ref[:, s] = mine[states:states + 1] * came + mine[:states]

            @pl.when(z == 0)
            def _():
                @pl.when(z < nz - 1)
                def _():
                    leave[:, s] = whole[:states]
                    push(ENTER, 3, c, leave, enter, me + PLANE).start()

                c_ref[:, s] = mine[:states]

        loop(body)
        loop(lambda c: push(FIRST, 0, c, first, first, me - 1).wait_send())

        @pl.when(z < nz - 1)
        def _():
            loop(lambda c: push(ENTER, 3, c, leave, enter, me + PLANE).wait_send())

        @pl.when(z > 0)
        def _():
            loop(lambda c: push(ENTER, 2, c, enter, enter, me - 2).wait_send())
            loop(lambda c: push(ENTER, 1, c, enter, enter, me - 1).wait_send())


def output_kernel(heads, width, states, sizes_ref, skip_ref, rate_ref, y_ref, d_ref, c_ref, t0_ref, o_ref):
    g = pl.program_id(0)
    tok = y_ref.shape[0]
    wx = heads * width
    starts = starts_of(sizes_ref)
    base = lax.axis_index("ctx") * tok
    rate = group_lanes(-jnp.exp(rate_ref[...]), g, heads)[0:1]
    carry = c_ref[...]
    for b in range(tok // BLOCK):
        lo = b * BLOCK
        first = base + lo
        dt = group_lanes(d_ref[lo:lo + BLOCK, :].astype(F32), g, heads)
        cum = decay_of(dt, rate)
        cum_t = cum.T
        dt_t = dt.T
        pos_i = first + lax.broadcasted_iota(jnp.int32, (BLOCK, BLOCK), 0)
        pos_j = first + lax.broadcasted_iota(jnp.int32, (BLOCK, BLOCK), 1)
        allowed = (pos_i >= pos_j) & (segment_of(pos_i, starts) == segment_of(pos_j, starts))
        row_pos = first + lax.broadcasted_iota(jnp.int32, (1, BLOCK), 1)
        cut = jnp.zeros((1, BLOCK), jnp.int32)
        for at in starts:
            cut = cut + ((row_pos >= at) & (at >= first)).astype(jnp.int32)
        opened = jnp.where(cut == 0, jnp.exp(cum_t[:heads]), 0.0)
        maps = y_ref[lo:lo + BLOCK, wx:]
        in_map = maps[:, :states]
        out_map = maps[:, states:]
        gram = dot_nt(out_map, in_map)
        x_fm = y_ref[lo:lo + BLOCK, :wx].T
        carried = dot_nt(carry.astype(BF16).T, out_map)
        for h in range(heads):
            gap = jnp.broadcast_to(cum[:, h:h + 1], (BLOCK, BLOCK)) - cum_t[h:h + 1]
            mask = jnp.exp(jnp.where(allowed, gap, -jnp.inf))
            mixing = (gram * (mask * dt_t[h:h + 1])).astype(BF16)
            r = slice(h * width, (h + 1) * width)
            xh = x_fm[r]
            res = dot_nt(xh, mixing) + carried[r] * opened[h:h + 1]
            res = res + skip_ref[g * heads + h] * xh.astype(F32)
            o_ref[r, lo:lo + BLOCK] = res.astype(BF16)
        if b < tok // BLOCK - 1:
            carry = t0_ref[b, states:states + 1, :] * carry + t0_ref[b, :states, :]


def per_device(n, inputs, projections, step_sizes, log_rates, skip_gain, packing, prompt_sizes):
    tok = inputs.shape[1]
    head_count = log_rates.shape[0]
    heads = head_count // G
    states = projections.shape[0] // (2 * G)
    width = inputs.shape[0] // head_count
    wx = heads * width
    wm = 2 * states
    slot = tok // n
    vmem = pl.BlockSpec(memory_space=pltpu.VMEM)
    smem = pl.BlockSpec(memory_space=pltpu.SMEM)
    sds = jax.ShapeDtypeStruct
    y, d = pl.pallas_call(
        prep_kernel,
        grid=(G,),
        in_specs=[
            pl.BlockSpec((1, tok), lambda g: (0, 0)),
            pl.BlockSpec((wx, tok), lambda g: (g, 0)),
            pl.BlockSpec((wm, tok), lambda g: (g, 0)),
            pl.BlockSpec((head_count, tok), lambda g: (0, 0)),
        ],
        out_specs=[
            pl.BlockSpec((tok, wx + wm), lambda g: (0, g)),
            pl.BlockSpec((tok, LANES), lambda g: (0, 0)),
        ],
        out_shape=[sds((tok, G * (wx + wm)), BF16), sds((tok, LANES), BF16)],
        name="prep",
    )(packing, inputs, projections, step_sizes)
    y = y.reshape(n, slot, G * (wx + wm))
    d = d.reshape(n, slot, LANES)
    y, d = pl.pallas_call(
        functools.partial(exchange_kernel, n),
        in_specs=[vmem, vmem],
        out_specs=[vmem, vmem],
        out_shape=[sds(y.shape, BF16), sds(d.shape, BF16)],
        scratch_shapes=[
            pltpu.SemaphoreType.DMA((2, n)),
            pltpu.SemaphoreType.DMA((2, n)),
            pltpu.SemaphoreType.DMA((2,)),
        ],
        compiler_params=pltpu.CompilerParams(collective_id=0, has_side_effects=True, vmem_limit_bytes=VLIM),
        name="exchange",
    )(y, d)
    y = y.reshape(tok, G * (wx + wm))
    d = d.reshape(tok, LANES)
    rates = jnp.pad(log_rates, (0, LANES - head_count)).reshape(1, LANES)
    rates = jnp.broadcast_to(rates, (8, LANES))
    blocks = tok // BLOCK
    rows = states + 8
    y_spec = pl.BlockSpec((tok, wx + wm), lambda g: (0, g))
    d_spec = pl.BlockSpec((tok, LANES), lambda g: (0, 0))
    r_spec = pl.BlockSpec((8, LANES), lambda g: (0, 0))
    t0_spec = pl.BlockSpec((blocks - 1, rows, wx), lambda g: (0, 0, g))
    t, t0 = pl.pallas_call(
        functools.partial(states_kernel, heads, width, states),
        grid=(G,),
        in_specs=[smem, r_spec, y_spec, d_spec],
        out_specs=[pl.BlockSpec((rows, wx), lambda g: (0, g)), t0_spec],
        out_shape=[sds((rows, G * wx), F32), sds((blocks - 1, rows, G * wx), F32)],
        name="states",
    )(prompt_sizes, rates, y, d)
    chunks = 8
    full = (rows, G * wx)
    only = (states, G * wx)
    carry = pl.pallas_call(
        functools.partial(chain_kernel, n, states, chunks),
        in_specs=[vmem],
        out_specs=vmem,
        out_shape=sds(only, F32),
        scratch_shapes=[
            pltpu.VMEM(full, F32),
            pltpu.VMEM(full, F32),
            pltpu.VMEM(full, F32),
            pltpu.VMEM(only, F32),
            pltpu.VMEM(only, F32),
            pltpu.SemaphoreType.DMA((4, chunks)),
            pltpu.SemaphoreType.DMA((3, chunks)),
        ],
        compiler_params=pltpu.CompilerParams(collective_id=1, has_side_effects=True, vmem_limit_bytes=VLIM),
        name="chain",
    )(t)
    return pl.pallas_call(
        functools.partial(output_kernel, heads, width, states),
        grid=(G,),
        in_specs=[smem, smem, r_spec, y_spec, d_spec,
                  pl.BlockSpec((states, wx), lambda g: (0, g)), t0_spec],
        out_specs=pl.BlockSpec((wx, tok), lambda g: (g, 0)),
        out_shape=sds((G * wx, tok), BF16),
        name="output",
    )(prompt_sizes, skip_gain, rates, y, d, carry, t0)


def solution(mesh):
    in_specs = (
        P(None, ("groups", "ctx")),
        P(None, ("groups", "ctx")),
        P(None, ("groups", "ctx")),
        P(),
        P(),
        P(("groups", "ctx"), None),
        P("groups"),
    )
    out_specs = P(None, ("groups", "ctx"))
    return jax.shard_map(
        functools.partial(per_device, mesh.shape["ctx"]),
        mesh=mesh, in_specs=in_specs, out_specs=out_specs, check_vma=False,
    )
```

time: 356 us -> 112 us (0.31)
  waiting for transfers between devices: 177 us -> 0 us
  Pallas kernels: 0 us -> 110 us
  other arithmetic: 54.9 us -> 0 us
  local copies, waits for them, and re-layouts: 42.3 us -> 1.26 us
  blocking collectives: 28.4 us -> 0 us
  starting transfers between devices: 18.6 us -> 0 us
  matrix products: 16 us -> 0 us
  between operations: 14.3 us -> 0.02 us
    all_gather x1 -> x0, waiting for transfers between devices: 140 us -> none  [carried_in(): pieces = jax.tree.map(lambda part: lax.all_gather(part, axis), value)]
    pallas_call x0 -> x5, Pallas kernels: none -> 110 us  [the longest x1 48.6 us: per_device(): pl.pallas_call(functools.partial(exchange_kernel, n), in_specs=[vmem, vme...]
    select_n x27 -> x0, other arithmetic: 37 us -> none  [the longest x15 31.1 us: lap(): jnp.where(position < mine, new, old)]
    all_to_all x3 -> x0, waiting for transfers between devices: 36.9 us -> none  [the longest x1 32.8 us: per_device(): lax.all_to_all(jnp.take(inputs, send_order, axis=1), 'ctx', split_axis=1,...]
    unnamed x1 -> x0, blocking collectives: 28.4 us -> none
    all_to_all x3 -> x0, starting transfers between devices: 18.5 us -> none  [the longest x1 6.43 us: per_device(): lax.all_to_all(jnp.take(inputs, send_order, axis=1), 'ctx', split_axis=1,...]
    dot_general x26 -> x0, matrix products: 16 us -> none  [the longest x8 9.38 us: group_part(): jnp.einsum('hpn,ni->hpi', carry_group.astype(jnp.bfloat16), output_map, p...]
    mul x31 -> x0, local copies, waits for them, and re-layouts: 13.4 us -> none  [the longest x15 10.4 us: combine(): later[0][:, None, None] * earlier[1] + later[1]]
  transfers between devices with their start and end apart: 4 -> 0, of which waited for: 3 -> 0; matrix products, arithmetic and copies ran while one was open for 7% -> 0% of each run, Pallas kernels for 0% -> 0%
where the time goes in v1:
time: 112 us
  Pallas kernels  110 us (98%)
  local copies, waits for them, and re-layouts  1.26 us (1%)
    pallas_call x1, Pallas kernels, per_device(): pl.pallas_call(functools.partial(exchange_kernel, n), in_specs=[vmem, vme...  48.6 us
    pallas_call x1, Pallas kernels, per_device(): pl.pallas_call(functools.partial(chain_kernel, n, states, chunks), in_spe...  40.2 us
    pallas_call x1, Pallas kernels, per_device(): pl.pallas_call(functools.partial(output_kernel, heads, width, states), gr...  8.92 us
    pallas_call x1, Pallas kernels, per_device(): pl.pallas_call(functools.partial(states_kernel, heads, width, states), gr...  8.05 us
    pallas_call x1, Pallas kernels, per_device(): pl.pallas_call(prep_kernel, grid=(G,), in_specs=[pl.BlockSpec((1, tok), l...  4.74 us

profile of v1, /device:TPU:26, one launch (start us, length us, event | category | flops | bytes accessed | tf_op | source)
XLA Modules:
  0.0 111.8 jit_solution(1005140517360824347)
XLA Ops:
  0.0 0.7 pad.4
  0.7 0.6 broadcast_in_dim.2.rate_ref
  1.3 4.7 %prep.1 = (bf16[256,4608]{1,0:T(8,128)(2,1)}, bf16[256,128]{1,0:T(8,128)(2,1)}) custom-call(s32[1,256]{1,0:T(1,128)} %pack_ref.1, bf16[4096,256]{1,0:T(8,128)(2,1)} %x_ref.1, bf16[512,256]{1,0:T(8,128)(2,1)} %bc_ref.1, bf16[64,256]{1,0:T(8,128)(2,1)} %dt_ref.1), custom_call_target="tpu_custom_call" | custom-call | tf_op jit(solution)/shard_map/prep/pallas_call | solution.py:414
  6.0 48.6 %exchange.1 = (bf16[16,16,4608]{2,1,0:T(8,128)(2,1)}, bf16[16,16,128]{2,1,0:T(8,128)(2,1)}) custom-call(bf16[16,16,4608]{2,1,0:T(8,128)(2,1)} %bitcast.6, bf16[16,16,128]{2,1,0:T(8,128)(2,1)} %bitcast.9), custom_call_target="tpu_custom_call" | custom-call | tf_op jit(solution)/shard_map/exchange/pallas_call | solution.py:432
  54.6 8.0 %states.1 = (f32[72,4096]{1,0:T(8,128)}, f32[1,72,4096]{2,1,0:T(8,128)}) custom-call(s32[4]{0:T(128)} %sizes_ref.3, f32[8,128]{1,0:T(8,128)} %broadcast_in_dim.2.rate_ref, bf16[256,4608]{1,0:T(8,128)(2,1)} %bitcast.4, bf16[256,128]{1,0:T(8,128)(2,1)} %bitcast.7), custom_call_target="tpu_custom_call" | custom-call | tf_op jit(solution)/shard_map/states/pallas_call | solution.py:455
  62.6 40.2 %chain.1.c_ref = f32[64,4096]{1,0:T(8,128)} custom-call(f32[72,4096]{1,0:T(8,128)} %get-tuple-element.15.t_ref), custom_call_target="tpu_custom_call" | custom-call | tf_op jit(solution)/shard_map/chain/pallas_call | solution.py:466
  102.9 8.9 %output.1 = bf16[4096,256]{1,0:T(8,128)(2,1)} custom-call(s32[4]{0:T(128)} %sizes_ref.3, f32[64]{0:T(128)} %skip_ref.1, f32[8,128]{1,0:T(8,128)} %broadcast_in_dim.2.rate_ref, bf16[256,4608]{1,0:T(8,128)(2,1)} %bitcast.5, bf16[256,128]{1,0:T(8,128)(2,1)} %bitcast.8, f32[64,4096]{1,0:T(8,128)} %chain.1.c_ref, f32[1,72,4096]{2,1,0:T(8,128)} %get-tuple-element.16.t0_ref), custom_call_target="tpu_custom_call" | custom-call | tf_op jit(solution)/shard_map/output/pallas_call | solution.py:483

commit v2 on v0

v2 whole, which is shorter than its diff:
```python
import functools
import jax
import jax.numpy as jnp
from jax import lax
from jax.experimental import pallas as pl
from jax.experimental.pallas import tpu as pltpu
from jax.sharding import PartitionSpec as P

G = 4
BLOCK = 128
LANES = 128
PLANE = 4
VLIM = 60 * 1024 * 1024
F32 = jnp.float32
BF16 = jnp.bfloat16
MESH = pl.DeviceIdType.MESH


def dot_nt(a, b):
    return lax.dot_general(a, b, (((1,), (1,)), ((), ())), preferred_element_type=F32)


def starts_of(sizes_ref):
    out = []
    at = jnp.int32(0)
    for s in range(sizes_ref.shape[0]):
        out.append(at)
        at = at + sizes_ref[s]
    return out


def segment_of(position, starts):
    seg = jnp.zeros(position.shape, jnp.int32)
    for at in starts:
        seg = seg + (position >= at).astype(jnp.int32)
    return seg


def decay_of(dt, rate):
    t = dt.shape[0]
    tri = jnp.where(
        lax.broadcasted_iota(jnp.int32, (t, t), 0) >= lax.broadcasted_iota(jnp.int32, (t, t), 1),
        1.0, 0.0).astype(F32)
    return jnp.dot(tri, dt * rate, preferred_element_type=F32, precision=lax.Precision.HIGHEST)


def spread(value, heads, width):
    rows = value.shape[0]
    per = LANES // width
    lane = lax.broadcasted_iota(jnp.int32, (rows, LANES), 1)
    out = []
    for q in range(heads // per):
        acc = jnp.broadcast_to(value[:, q * per:q * per + 1], (rows, LANES))
        for k in range(1, per):
            other = jnp.broadcast_to(value[:, q * per + k:q * per + k + 1], (rows, LANES))
            acc = jnp.where(lane >= k * width, other, acc)
        out.append(acc)
    return jnp.concatenate(out, axis=1)


def group_lanes(value, g, per_group):
    return pltpu.roll(value, lax.rem(LANES - g * per_group, LANES), 1)


def fused_kernel(
    n, heads, width, states, sub,
    sizes_ref, skip_ref, rate_ref, pack_ref, x_hbm, bc_hbm, dt_ref, o_hbm,
    xv, bv, pick, ys, yr, ds, dr, cums, dts, acc, opens, obuf,
    t_ref, t0_ref, early, first, mine, whole, leave, enter, c_ref,
    in_sem, out_sem, own_sem, own_d_sem, xs_sem, xr_sem, dsend_sem, drecv_sem, ssem, rsem,
):
    me = lax.axis_index("ctx")
    tok = dt_ref.shape[1]
    slot = tok // n
    wx = heads * width
    wm = 2 * states
    blocks = tok // BLOCK
    half = n // 2
    q = lax.rem(me, PLANE)
    z = me // PLANE
    nz = n // PLANE
    cw = wx // sub
    starts = starts_of(sizes_ref)
    base = me * tok

    def loop(count, body, low=0):
        def step(i, _):
            body(i)
            return 0
        lax.fori_loop(low, count, step, 0)

    barrier = pltpu.get_barrier_semaphore()
    loop(n, lambda off: pl.semaphore_signal(
        barrier, inc=1, device_id={"ctx": lax.rem(me + off, n)}, device_id_type=MESH), low=1)

    def load(g):
        rx = pl.ds(pl.multiple_of(g * wx, LANES), wx)
        rb = pl.ds(pl.multiple_of(g * wm, LANES), wm)
        return (
            pltpu.make_async_copy(x_hbm.at[rx], xv.at[g], in_sem.at[0, g]),
            pltpu.make_async_copy(bc_hbm.at[rb], bv.at[g], in_sem.at[1, g]),
        )

    def begin(g):
        for part in load(g):
            part.start()

    loop(G, begin)

    rows = lax.broadcasted_iota(jnp.int32, (tok, tok), 0)
    pick[...] = jnp.where(rows == pack_ref[...], 1.0, 0.0).astype(F32).T.astype(BF16)
    head_count = dt_ref.shape[0]
    dt_all = dot_nt(pick[...], dt_ref[...]).astype(BF16)
    dt_all = jnp.concatenate([dt_all, jnp.zeros((tok, LANES - head_count), BF16)], axis=1)
    ds[...] = dt_all.reshape(n, slot, LANES)

    def prep(g):
        for part in load(g):
            part.wait()
        yx = dot_nt(pick[...], xv[g]).astype(BF16)
        yb = dot_nt(pick[...], bv[g]).astype(BF16)
        ys[g, :, :, :wx] = yx.reshape(n, slot, wx)
        ys[g, :, :, wx:] = yb.reshape(n, slot, wm)

    def send_y(g, off):
        to = lax.rem(me + off, n)
        return pltpu.make_async_remote_copy(
            ys.at[g, to], yr.at[g, me], xs_sem.at[g, off], xr_sem.at[g, off],
            device_id={"ctx": to}, device_id_type=MESH)

    def send_d(off):
        to = lax.rem(me + off, n)
        return pltpu.make_async_remote_copy(
            ds.at[to], dr.at[me], dsend_sem.at[off], drecv_sem.at[off],
            device_id={"ctx": to}, device_id_type=MESH)

    def keep_y(g):
        return pltpu.make_async_copy(ys.at[g, me], yr.at[g, me], own_sem.at[g])

    def keep_d():
        return pltpu.make_async_copy(ds.at[me], dr.at[me], own_d_sem.at[0])

    def send_all(g):
        def pair(i):
            send_y(g, half - i).start()

            @pl.when(i > 0)
            def _():
                send_y(g, half + i).start()

        loop(half, pair)
        keep_y(g).start()

    prep(0)
    pl.semaphore_wait(barrier, n - 1)
    loop(n, lambda off: send_d(off).start(), low=1)
    keep_d().start()

    def prep_next(g):
        @pl.when(g < G - 1)
        def _():
            prep(g + 1)
        send_all(g)

    loop(G, prep_next)

    def push(kind, way, g, k, src, dst, to):
        s = pl.ds(pl.multiple_of(k * cw, LANES), cw)
        return pltpu.make_async_remote_copy(
            src.at[g, :, s], dst.at[g, :, s], ssem.at[way, g, k], rsem.at[kind, g, k],
            device_id={"ctx": to}, device_id_type=MESH)

    EARLY, FIRST, ENTER = 0, 1, 2

    def lanes(k):
        return pl.ds(pl.multiple_of(k * cw, LANES), cw)

    def join(old, new):
        gain = new[states:states + 1]
        return jnp.concatenate([gain * old[:states] + new[:states], old[states:] * new[states:]], axis=0)

    def local_stage(g):
        @pl.when((q == 0) | (q == 2))
        def _():
            loop(sub, lambda k: push(EARLY, 0, g, k, t_ref, early, me + 1).start())

        @pl.when(q == 1)
        def _():
            def up(k):
                s = lanes(k)
                push(EARLY, 0, g, k, t_ref, early, me - 1).wait_recv()
                whole[g, :, s] = join(early[g, :, s], t_ref[g, :, s])
                push(FIRST, 0, g, k, whole, first, me + 2).start()
            loop(sub, up)

        @pl.when(q == 3)
        def _():
            def up(k):
                s = lanes(k)
                push(EARLY, 0, g, k, t_ref, early, me - 1).wait_recv()
                push(FIRST, 0, g, k, first, first, me - 1).wait_recv()
                push(FIRST, 0, g, k, first, first, me - 1).start()
                both = join(first[g, :, s], early[g, :, s])
                mine[:, s] = both
                every = join(both, t_ref[g, :, s])
                whole[g, :, s] = every

                @pl.when((z == 0) & (nz > 1))
                def _():
                    leave[g, :, s] = every[:states]
                    push(ENTER, 3, g, k, leave, enter, me + PLANE).start()
            loop(sub, up)

    def carry_stage(g):
        def merge(local, k):
            s = lanes(k)

            @pl.when(z > 0)
            def _():
                c_ref[:, s] = local[states:states + 1] * enter[g, :, s] + local[:states]

            @pl.when(z == 0)
            def _():
                c_ref[:, s] = local[:states]

        @pl.when(q == 0)
        def _():
            def body(k):
                s = lanes(k)

                @pl.when(z > 0)
                def _():
                    push(ENTER, 1, g, k, enter, enter, me + 1).wait_recv()
                    c_ref[:, s] = enter[g, :, s]

                @pl.when(z == 0)
                def _():
                    c_ref[:, s] = jnp.zeros((states, cw), F32)
            loop(sub, body)

        @pl.when(q == 1)
        def _():
            def body(k):
                @pl.when(z > 0)
                def _():
                    push(ENTER, 1, g, k, enter, enter, me - 1).wait_recv()
                    push(ENTER, 1, g, k, enter, enter, me - 1).start()
                merge(early[g, :, lanes(k)], k)
            loop(sub, body)

        @pl.when(q == 2)
        def _():
            def body(k):
                push(FIRST, 1, g, k, first, first, me + 1).wait_recv()

                @pl.when(z > 0)
                def _():
                    push(ENTER, 1, g, k, enter, enter, me + 1).wait_recv()
                merge(first[g, :, lanes(k)], k)
            loop(sub, body)

        @pl.when(q == 3)
        def _():
            def body(k):
                s = lanes(k)

                @pl.when(z > 0)
                def _():
                    push(ENTER, 1, g, k, enter, enter, me - 1).wait_recv()

                    @pl.when(z < nz - 1)
                    def _():
                        leave[g, :, s] = (
                            whole[g, states:states + 1, s] * enter[g, :, s] + whole[g, :states, s])
                        push(ENTER, 3, g, k, leave, enter, me + PLANE).start()

                    push(ENTER, 2, g, k, enter, enter, me - 2).start()
                    push(ENTER, 1, g, k, enter, enter, me - 1).start()
                merge(mine[:, s], k)
            loop(sub, body)

    def settle(g):
        def one(k):
            @pl.when((q == 0) | (q == 2))
            def _():
                push(EARLY, 0, g, k, t_ref, early, me + 1).wait_send()

            @pl.when(q == 1)
            def _():
                push(FIRST, 0, g, k, whole, first, me + 2).wait_send()

                @pl.when(z > 0)
                def _():
                    push(ENTER, 1, g, k, enter, enter, me - 1).wait_send()

            @pl.when(q == 3)
            def _():
                push(FIRST, 0, g, k, first, first, me - 1).wait_send()

                @pl.when(z < nz - 1)
                def _():
                    push(ENTER, 3, g, k, leave, enter, me + PLANE).wait_send()

                @pl.when(z > 0)
                def _():
                    push(ENTER, 2, g, k, enter, enter, me - 2).wait_send()
                    push(ENTER, 1, g, k, enter, enter, me - 1).wait_send()
        loop(sub, one)

    rate_all = jnp.concatenate(
        [rate_ref[...], jnp.zeros((1, LANES - head_count), F32)], axis=1)
    rate_all = jnp.broadcast_to(-jnp.exp(rate_all), (8, LANES))

    def rows_of(b):
        return slice(b * BLOCK // slot, (b + 1) * BLOCK // slot)

    def y_of(g, b, lo, hi):
        return yr[g, rows_of(b), :, lo:hi].reshape(BLOCK, hi - lo)

    def states_stage(g):
        rate = group_lanes(rate_all, g, heads)[0:1]
        total = None
        for b in range(blocks):
            lo = b * BLOCK
            head = base + lo
            last = head + BLOCK - 1
            dt = dr[rows_of(b)].reshape(BLOCK, LANES).astype(F32)
            dt = group_lanes(dt, g, heads)
            cum = decay_of(dt, rate)
            cums[lo:lo + BLOCK, :] = cum
            dts[lo:lo + BLOCK, :] = dt
            end = cum[BLOCK - 1:BLOCK, :]
            pos = head + lax.broadcasted_iota(jnp.int32, (BLOCK, LANES), 0)
            last_seg = jnp.int32(0)
            cut = jnp.int32(0)
            for at in starts:
                last_seg = last_seg + (last >= at).astype(jnp.int32)
                cut = cut + ((at >= head) & (at <= last)).astype(jnp.int32)
            same = segment_of(pos, starts) == last_seg
            into = jnp.where(same, jnp.exp(end - cum), 0.0) * dt
            weighted = (y_of(g, b, 0, wx).astype(F32) * spread(into, heads, width)).astype(BF16)
            maps_t = y_of(g, b, wx, wx + wm).astype(F32).T
            in_map = maps_t[:states].astype(BF16)
            block_total = jnp.dot(in_map, weighted, preferred_element_type=F32)
            keep_h = jnp.where(cut == 0, jnp.exp(end), 0.0)
            keep = spread(jnp.broadcast_to(keep_h, (8, LANES)), heads, width)
            if total is None:
                total, gain = block_total, keep
            else:
                total = keep[0:1] * total + block_total
                gain = gain * keep
            if b < blocks - 1:
                t0_ref[b, :states, :] = block_total
                t0_ref[b, states:, :] = keep
        t_ref[g, :states, :] = total
        t_ref[g, states:, :] = gain

    def inner_stage(g):
        for b in range(blocks):
            lo = b * BLOCK
            head = base + lo
            cum = cums[lo:lo + BLOCK, :]
            cum_t = cum.T
            dt_t = dts[lo:lo + BLOCK, :].T
            pos_i = head + lax.broadcasted_iota(jnp.int32, (BLOCK, BLOCK), 0)
            pos_j = head + lax.broadcasted_iota(jnp.int32, (BLOCK, BLOCK), 1)
            allowed = (pos_i >= pos_j) & (segment_of(pos_i, starts) == segment_of(pos_j, starts))
            row_pos = head + lax.broadcasted_iota(jnp.int32, (1, BLOCK), 1)
            cut = jnp.zeros((1, BLOCK), jnp.int32)
            for at in starts:
                cut = cut + ((row_pos >= at) & (at >= head)).astype(jnp.int32)
            opens[b] = jnp.where(cut == 0, jnp.exp(cum_t[:heads]), 0.0)
            in_map = y_of(g, b, wx, wx + states)
            out_map = y_of(g, b, wx + states, wx + wm)
            gram = dot_nt(out_map, in_map)
            x_fm = y_of(g, b, 0, wx).T
            for h in range(heads):
                gap = jnp.broadcast_to(cum[:, h:h + 1], (BLOCK, BLOCK)) - cum_t[h:h + 1]
                mask = jnp.exp(jnp.where(allowed, gap, -jnp.inf))
                mixing = (gram * (mask * dt_t[h:h + 1])).astype(BF16)
                r = slice(h * width, (h + 1) * width)
                xh = x_fm[r]
                acc[r, lo:lo + BLOCK] = (
                    dot_nt(xh, mixing) + skip_ref[g * heads + h] * xh.astype(F32))

    def store_out(g):
        return pltpu.make_async_copy(
            obuf.at[g], o_hbm.at[pl.ds(pl.multiple_of(g * wx, LANES), wx)], out_sem.at[g])

    def output_stage(g):
        carry = c_ref[...]
        for b in range(blocks):
            lo = b * BLOCK
            out_map = y_of(g, b, wx + states, wx + wm)
            carried = dot_nt(carry.astype(BF16).T, out_map)
            for h in range(heads):
                r = slice(h * width, (h + 1) * width)
                obuf[g, r, lo:lo + BLOCK] = (
                    acc[r, lo:lo + BLOCK] + carried[r] * opens[b, h:h + 1]).astype(BF16)
            if b < blocks - 1:
                carry = t0_ref[b, states:states + 1, :] * carry + t0_ref[b, :states, :]
        store_out(g).start()

    loop(n, lambda off: send_d(off).wait_recv(), low=1)
    keep_d().wait()

    def turn(g):
        loop(n, lambda off: send_y(g, off).wait_recv(), low=1)
        keep_y(g).wait()
        states_stage(g)
        local_stage(g)
        inner_stage(g)
        carry_stage(g)
        output_stage(g)

    loop(G, turn)
    loop(n, lambda off: send_d(off).wait_send(), low=1)

    def close(g):
        loop(n, lambda off: send_y(g, off).wait_send(), low=1)
        settle(g)
        store_out(g).wait()

    loop(G, close)


def per_device(n, inputs, projections, step_sizes, log_rates, skip_gain, packing, prompt_sizes):
    tok = inputs.shape[1]
    head_count = log_rates.shape[0]
    heads = head_count // G
    states = projections.shape[0] // (2 * G)
    width = inputs.shape[0] // head_count
    wx = heads * width
    wm = 2 * states
    slot = tok // n
    blocks = tok // BLOCK
    rows = states + 8
    sub = 4
    vmem = pl.BlockSpec(memory_space=pltpu.VMEM)
    smem = pl.BlockSpec(memory_space=pltpu.SMEM)
    hbm = pl.BlockSpec(memory_space=pl.ANY)
    dma = pltpu.SemaphoreType.DMA
    return pl.pallas_call(
        functools.partial(fused_kernel, n, heads, width, states, sub),
        in_specs=[smem, smem, vmem, vmem, hbm, hbm, vmem],
        out_specs=hbm,
        out_shape=jax.ShapeDtypeStruct((G * wx, tok), BF16),
        scratch_shapes=[
            pltpu.VMEM((G, wx, tok), BF16),
            pltpu.VMEM((G, wm, tok), BF16),
            pltpu.VMEM((tok, tok), BF16),
            pltpu.VMEM((G, n, slot, wx + wm), BF16),
            pltpu.VMEM((G, n, slot, wx + wm), BF16),
            pltpu.VMEM((n, slot, LANES), BF16),
            pltpu.VMEM((n, slot, LANES), BF16),
            pltpu.VMEM((tok, LANES), F32),
            pltpu.VMEM((tok, LANES), F32),
            pltpu.VMEM((wx, tok), F32),
            pltpu.VMEM((blocks, heads, BLOCK), F32),
            pltpu.VMEM((G, wx, tok), BF16),
            pltpu.VMEM((G, rows, wx), F32),
            pltpu.VMEM((blocks - 1, rows, wx), F32),
            pltpu.VMEM((G, rows, wx), F32),
            pltpu.VMEM((G, rows, wx), F32),
            pltpu.VMEM((rows, wx), F32),
            pltpu.VMEM((G, rows, wx), F32),
            pltpu.VMEM((G, states, wx), F32),
            pltpu.VMEM((G, states, wx), F32),
            pltpu.VMEM((states, wx), F32),
            dma((2, G)),
            dma((G,)),
            dma((G,)),
            dma((1,)),
            dma((G, n)),
            dma((G, n)),
            dma((n,)),
            dma((n,)),
            dma((4, G, sub)),
            dma((3, G, sub)),
        ],
        compiler_params=pltpu.CompilerParams(
            collective_id=0, has_side_effects=True, vmem_limit_bytes=VLIM),
        name="prefill",
    )(prompt_sizes, skip_gain, log_rates.reshape(1, head_count), packing,
      inputs, projections, step_sizes)


def solution(mesh):
    in_specs = (
        P(None, ("groups", "ctx")),
        P(None, ("groups", "ctx")),
        P(None, ("groups", "ctx")),
        P(),
        P(),
        P(("groups", "ctx"), None),
        P("groups"),
    )
    out_specs = P(None, ("groups", "ctx"))
    return jax.shard_map(
        functools.partial(per_device, mesh.shape["ctx"]),
        mesh=mesh, in_specs=in_specs, out_specs=out_specs, check_vma=False,
    )
```

time: 356 us -> 116 us (0.33); the launches traced: 352 us -> 116 us
  waiting for transfers between devices: 177 us -> 0 us
  Pallas kernels: 0 us -> 113 us
  other arithmetic: 54.9 us -> 0 us
  local copies, waits for them, and re-layouts: 42.3 us -> 3.05 us
  blocking collectives: 28.4 us -> 0 us
  starting transfers between devices: 18.6 us -> 0 us
  matrix products: 16 us -> 0 us
  between operations: 14.3 us -> 0.01 us
    all_gather x1 -> x0, waiting for transfers between devices: 140 us -> none  [carried_in(): pieces = jax.tree.map(lambda part: lax.all_gather(part, axis), value)]
    pallas_call x0 -> x1, Pallas kernels: none -> 113 us  [per_device(): pl.pallas_call(functools.partial(fused_kernel, n, heads, width, states, s...]
    select_n x27 -> x0, other arithmetic: 37 us -> none  [the longest x15 31.1 us: lap(): jnp.where(position < mine, new, old)]
    all_to_all x3 -> x0, waiting for transfers between devices: 36.9 us -> none  [the longest x1 32.8 us: per_device(): lax.all_to_all(jnp.take(inputs, send_order, axis=1), 'ctx', split_axis=1,...]
    unnamed x1 -> x0, blocking collectives: 28.4 us -> none
    all_to_all x3 -> x0, starting transfers between devices: 18.5 us -> none  [the longest x1 6.43 us: per_device(): lax.all_to_all(jnp.take(inputs, send_order, axis=1), 'ctx', split_axis=1,...]
    dot_general x26 -> x0, matrix products: 16 us -> none  [the longest x8 9.38 us: group_part(): jnp.einsum('hpn,ni->hpi', carry_group.astype(jnp.bfloat16), output_map, p...]
    mul x31 -> x0, local copies, waits for them, and re-layouts: 13.4 us -> none  [the longest x15 10.4 us: combine(): later[0][:, None, None] * earlier[1] + later[1]]
  transfers between devices with their start and end apart: 4 -> 0, of which waited for: 3 -> 0; matrix products, arithmetic and copies ran while one was open for 7% -> 0% of each run, Pallas kernels for 0% -> 0%
where the time goes in v2:
time: 116 us
  Pallas kernels  113 us (97%)
  local copies, waits for them, and re-layouts  3.05 us (3%)
    pallas_call x1, Pallas kernels, per_device(): pl.pallas_call(functools.partial(fused_kernel, n, heads, width, states, s...  113 us
    unnamed x1, local copies, waits for them, and re-layouts  3.05 us

profile of v2, /device:TPU:26, one launch (start us, length us, event | category | flops | bytes accessed | tf_op | source)
XLA Modules:
  0.0 116.1 jit_solution(5830538843096189621)
XLA Ops:
  0.0 113.1 %prefill.1 = bf16[4096,256]{1,0:T(8,128)(2,1)} custom-call(s32[4]{0:T(128)} %sizes_ref.1, f32[64]{0:T(128)} %skip_ref.1, f32[1,64]{1,0:T(1,128)} %bitcast.1, s32[1,256]{1,0:T(1,128)} %pack_ref.1, bf16[4096,256]{1,0:T(8,128)(2,1)} %x_hbm.1, bf16[512,256]{1,0:T(8,128)(2,1)} %bc_hbm.1, bf16[64,256]{1,0:T(8,128)(2,1)} %dt_ref.1), custom_call_target="tpu_custom_call" | custom-call | tf_op jit(solution)/shard_map/prefill/pallas_call | solution.py:443
  113.1 3.0 %copy.9 = bf16[4096,256]{1,0:T(8,128)(2,1)} copy(bf16[4096,256]{1,0:T(8,128)(2,1)} %prefill.1) | data formatting | bytes 4194304

commit v3 on v2

--- a/solution.py
+++ b/solution.py
@@ -179,11 +179,12 @@
         gain = new[states:states + 1]
         return jnp.concatenate([gain * old[:states] + new[:states], old[states:] * new[states:]], axis=0)
 
+    def open_stage(g):
+        @pl.when((q == 0) | (q == 2))
+        def _():
+            loop(sub, lambda k: push(EARLY, 0, g, k, t_ref, early, me + 1).start())
+
     def local_stage(g):
-        @pl.when((q == 0) | (q == 2))
-        def _():
-            loop(sub, lambda k: push(EARLY, 0, g, k, t_ref, early, me + 1).start())
-
         @pl.when(q == 1)
         def _():
             def up(k):
@@ -201,7 +202,7 @@
                 push(FIRST, 0, g, k, first, first, me - 1).wait_recv()
                 push(FIRST, 0, g, k, first, first, me - 1).start()
                 both = join(first[g, :, s], early[g, :, s])
-                mine[:, s] = both
+                mine[g, :, s] = both
                 every = join(both, t_ref[g, :, s])
                 whole[g, :, s] = every
 
@@ -217,11 +218,11 @@
 
             @pl.when(z > 0)
             def _():
-                c_ref[:, s] = local[states:states + 1] * enter[g, :, s] + local[:states]
+                c_ref[g, :, s] = local[states:states + 1] * enter[g, :, s] + local[:states]
 
             @pl.when(z == 0)
             def _():
-                c_ref[:, s] = local[:states]
+                c_ref[g, :, s] = local[:states]
 
         @pl.when(q == 0)
         def _():
@@ -231,11 +232,11 @@
                 @pl.when(z > 0)
                 def _():
                     push(ENTER, 1, g, k, enter, enter, me + 1).wait_recv()
-                    c_ref[:, s] = enter[g, :, s]
+                    c_ref[g, :, s] = enter[g, :, s]
 
                 @pl.when(z == 0)
                 def _():
-                    c_ref[:, s] = jnp.zeros((states, cw), F32)
+                    c_ref[g, :, s] = jnp.zeros((states, cw), F32)
             loop(sub, body)
 
         @pl.when(q == 1)
@@ -276,7 +277,7 @@
 
                     push(ENTER, 2, g, k, enter, enter, me - 2).start()
                     push(ENTER, 1, g, k, enter, enter, me - 1).start()
-                merge(mine[:, s], k)
+                merge(mine[g, :, s], k)
             loop(sub, body)
 
     def settle(g):
@@ -350,8 +351,8 @@
                 total = keep[0:1] * total + block_total
                 gain = gain * keep
             if b < blocks - 1:
-                t0_ref[b, :states, :] = block_total
-                t0_ref[b, states:, :] = keep
+                t0_ref[g, b, :states, :] = block_total
+                t0_ref[g, b, states:, :] = keep
         t_ref[g, :states, :] = total
         t_ref[g, states:, :] = gain
 
@@ -369,7 +370,7 @@
             cut = jnp.zeros((1, BLOCK), jnp.int32)
             for at in starts:
                 cut = cut + ((row_pos >= at) & (at >= head)).astype(jnp.int32)
-            opens[b] = jnp.where(cut == 0, jnp.exp(cum_t[:heads]), 0.0)
+            opens[g, b] = jnp.where(cut == 0, jnp.exp(cum_t[:heads]), 0.0)
             in_map = y_of(g, b, wx, wx + states)
             out_map = y_of(g, b, wx + states, wx + wm)
             gram = dot_nt(out_map, in_map)
@@ -380,7 +381,7 @@
                 mixing = (gram * (mask * dt_t[h:h + 1])).astype(BF16)
                 r = slice(h * width, (h + 1) * width)
                 xh = x_fm[r]
-                acc[r, lo:lo + BLOCK] = (
+                acc[g, r, lo:lo + BLOCK] = (
                     dot_nt(xh, mixing) + skip_ref[g * heads + h] * xh.astype(F32))
 
     def store_out(g):
@@ -388,7 +389,7 @@
             obuf.at[g], o_hbm.at[pl.ds(pl.multiple_of(g * wx, LANES), wx)], out_sem.at[g])
 
     def output_stage(g):
-        carry = c_ref[...]
+        carry = c_ref[g]
         for b in range(blocks):
             lo = b * BLOCK
             out_map = y_of(g, b, wx + states, wx + wm)
@@ -396,24 +397,49 @@
             for h in range(heads):
                 r = slice(h * width, (h + 1) * width)
                 obuf[g, r, lo:lo + BLOCK] = (
-                    acc[r, lo:lo + BLOCK] + carried[r] * opens[b, h:h + 1]).astype(BF16)
+                    acc[g, r, lo:lo + BLOCK] + carried[r] * opens[g, b, h:h + 1]).astype(BF16)
             if b < blocks - 1:
-                carry = t0_ref[b, states:states + 1, :] * carry + t0_ref[b, :states, :]
+                carry = t0_ref[g, b, states:states + 1, :] * carry + t0_ref[g, b, :states, :]
         store_out(g).start()
 
     loop(n, lambda off: send_d(off).wait_recv(), low=1)
     keep_d().wait()
 
+    ahead = z < nz // 2
+
     def turn(g):
+        @pl.when(ahead & (g == G - 1))
+        def _():
+            loop(G - 1, carry_stage)
+
         loop(n, lambda off: send_y(g, off).wait_recv(), low=1)
         keep_y(g).wait()
         states_stage(g)
-        local_stage(g)
+        open_stage(g)
+
+        @pl.when(g == G - 1)
+        def _():
+            local_stage(g)
+
         inner_stage(g)
-        carry_stage(g)
+
+        @pl.when(g < G - 1)
+        def _():
+            local_stage(g)
+
+    loop(G, turn)
+
+    @pl.when(ahead)
+    def _():
+        carry_stage(G - 1)
+
+    def wrap(g):
+        @pl.when(jnp.logical_not(ahead))
+        def _():
+            carry_stage(g)
         output_stage(g)
 
-    loop(G, turn)
+    loop(G, wrap)
     loop(n, lambda off: send_d(off).wait_send(), low=1)
 
     def close(g):
@@ -455,18 +481,18 @@
             pltpu.VMEM((n, slot, LANES), BF16),
             pltpu.VMEM((tok, LANES), F32),
             pltpu.VMEM((tok, LANES), F32),
-            pltpu.VMEM((wx, tok), F32),
-            pltpu.VMEM((blocks, heads, BLOCK), F32),
+            pltpu.VMEM((G, wx, tok), F32),
+            pltpu.VMEM((G, blocks, heads, BLOCK), F32),
             pltpu.VMEM((G, wx, tok), BF16),
             pltpu.VMEM((G, rows, wx), F32),
-            pltpu.VMEM((blocks - 1, rows, wx), F32),
+            pltpu.VMEM((G, blocks - 1, rows, wx), F32),
             pltpu.VMEM((G, rows, wx), F32),
             pltpu.VMEM((G, rows, wx), F32),
-            pltpu.VMEM((rows, wx), F32),
+            pltpu.VMEM((G, rows, wx), F32),
             pltpu.VMEM((G, rows, wx), F32),
             pltpu.VMEM((G, states, wx), F32),
             pltpu.VMEM((G, states, wx), F32),
-            pltpu.VMEM((states, wx), F32),
+            pltpu.VMEM((G, states, wx), F32),
             dma((2, G)),
             dma((G,)),
             dma((G,)),

time: 116 us -> 95.7 us (0.83)
  Pallas kernels: 113 us -> 92.5 us
    pallas_call x1, Pallas kernels: 113 us -> 92.5 us  [per_device(): pl.pallas_call(functools.partial(fused_kernel, n, heads, width, states, s...]
where the time goes in v3:
time: 95.7 us; the launch traced here: 95.5 us
  Pallas kernels  92.5 us (97%)
  local copies, waits for them, and re-layouts  3.05 us (3%)
    pallas_call x1, Pallas kernels, per_device(): pl.pallas_call(functools.partial(fused_kernel, n, heads, width, states, s...  92.5 us
    unnamed x1, local copies, waits for them, and re-layouts  3.05 us

profile of v3, /device:TPU:26, one launch (start us, length us, event | category | flops | bytes accessed | tf_op | source)
XLA Modules:
  0.0 95.5 jit_solution(7637449038671613034)
XLA Ops:
  0.0 92.5 %prefill.1 = bf16[4096,256]{1,0:T(8,128)(2,1)} custom-call(s32[4]{0:T(128)} %sizes_ref.1, f32[64]{0:T(128)} %skip_ref.1, f32[1,64]{1,0:T(1,128)} %bitcast.1, s32[1,256]{1,0:T(1,128)} %pack_ref.1, bf16[4096,256]{1,0:T(8,128)(2,1)} %x_hbm.1, bf16[512,256]{1,0:T(8,128)(2,1)} %bc_hbm.1, bf16[64,256]{1,0:T(8,128)(2,1)} %dt_ref.1), custom_call_target="tpu_custom_call" | custom-call | tf_op jit(solution)/shard_map/prefill/pallas_call | solution.py:469
  92.5 3.0 %copy.9 = bf16[4096,256]{1,0:T(8,128)(2,1)} copy(bf16[4096,256]{1,0:T(8,128)(2,1)} %prefill.1) | data formatting | bytes 4194304

commit v4 on v3

--- a/solution.py
+++ b/solution.py
@@ -10,7 +10,7 @@
 BLOCK = 128
 LANES = 128
 PLANE = 4
-VLIM = 60 * 1024 * 1024
+VLIM = 36 * 1024 * 1024
 F32 = jnp.float32
 BF16 = jnp.bfloat16
 MESH = pl.DeviceIdType.MESH
@@ -64,10 +64,11 @@
 
 def fused_kernel(
     n, heads, width, states, sub,
-    sizes_ref, skip_ref, rate_ref, pack_ref, x_hbm, bc_hbm, dt_ref, o_hbm,
+    sizes_hbm, skip_hbm, rate_hbm, pack_hbm, x_hbm, bc_hbm, dt_hbm, o_hbm,
+    sizes_ref, skip_ref, rate_ref, pack_ref, dt_ref,
     xv, bv, pick, ys, yr, ds, dr, cums, dts, acc, opens, obuf,
     t_ref, t0_ref, early, first, mine, whole, leave, enter, c_ref,
-    in_sem, out_sem, own_sem, own_d_sem, xs_sem, xr_sem, dsend_sem, drecv_sem, ssem, rsem,
+    in_sem, few_sem, out_sem, own_sem, own_d_sem, xs_sem, xr_sem, dsend_sem, drecv_sem, ssem, rsem,
 ):
     me = lax.axis_index("ctx")
     tok = dt_ref.shape[1]
@@ -80,7 +81,6 @@
     z = me // PLANE
     nz = n // PLANE
     cw = wx // sub
-    starts = starts_of(sizes_ref)
     base = me * tok
 
     def loop(count, body, low=0):
@@ -105,11 +105,23 @@
         for part in load(g):
             part.start()
 
+    few = [
+        pltpu.make_async_copy(src, dst, few_sem.at[i])
+        for i, (src, dst) in enumerate((
+            (pack_hbm, pack_ref), (dt_hbm, dt_ref), (sizes_hbm, sizes_ref),
+            (skip_hbm, skip_ref), (rate_hbm, rate_ref)))
+    ]
+    few[0].start()
+    few[1].start()
     loop(G, begin)
+    for part in few[2:]:
+        part.start()
+    few[0].wait()
 
     rows = lax.broadcasted_iota(jnp.int32, (tok, tok), 0)
     pick[...] = jnp.where(rows == pack_ref[...], 1.0, 0.0).astype(F32).T.astype(BF16)
     head_count = dt_ref.shape[0]
+    few[1].wait()
     dt_all = dot_nt(pick[...], dt_ref[...]).astype(BF16)
     dt_all = jnp.concatenate([dt_all, jnp.zeros((tok, LANES - head_count), BF16)], axis=1)
     ds[...] = dt_all.reshape(n, slot, LANES)
@@ -308,6 +320,9 @@
                     push(ENTER, 1, g, k, enter, enter, me - 1).wait_send()
         loop(sub, one)
 
+    for part in few[2:]:
+        part.wait()
+    starts = starts_of(sizes_ref)
     rate_all = jnp.concatenate(
         [rate_ref[...], jnp.zeros((1, LANES - head_count), F32)], axis=1)
     rate_all = jnp.broadcast_to(-jnp.exp(rate_all), (8, LANES))
@@ -405,7 +420,8 @@
     loop(n, lambda off: send_d(off).wait_recv(), low=1)
     keep_d().wait()
 
-    ahead = z < nz // 2
+    final = z == nz - 1
+    ahead = (z < nz // 2) & jnp.logical_not(final)
 
     def turn(g):
         @pl.when(ahead & (g == G - 1))
@@ -421,6 +437,10 @@
         def _():
             local_stage(g)
 
+            @pl.when(jnp.logical_not(final))
+            def _():
+                loop(G, carry_stage, low=jnp.where(ahead, G - 1, 0))
+
         inner_stage(g)
 
         @pl.when(g < G - 1)
@@ -429,12 +449,8 @@
 
     loop(G, turn)
 
-    @pl.when(ahead)
-    def _():
-        carry_stage(G - 1)
-
     def wrap(g):
-        @pl.when(jnp.logical_not(ahead))
+        @pl.when(final)
         def _():
             carry_stage(g)
         output_stage(g)
@@ -462,16 +478,19 @@
     blocks = tok // BLOCK
     rows = states + 8
     sub = 4
-    vmem = pl.BlockSpec(memory_space=pltpu.VMEM)
-    smem = pl.BlockSpec(memory_space=pltpu.SMEM)
-    hbm = pl.BlockSpec(memory_space=pl.ANY)
+    hbm = pl.BlockSpec(memory_space=pltpu.HBM)
     dma = pltpu.SemaphoreType.DMA
     return pl.pallas_call(
         functools.partial(fused_kernel, n, heads, width, states, sub),
-        in_specs=[smem, smem, vmem, vmem, hbm, hbm, vmem],
-        out_specs=hbm,
+        in_specs=[hbm] * 7,
+        out_specs=pl.BlockSpec(memory_space=pl.ANY),
         out_shape=jax.ShapeDtypeStruct((G * wx, tok), BF16),
         scratch_shapes=[
+            pltpu.SMEM(prompt_sizes.shape, jnp.int32),
+            pltpu.SMEM(skip_gain.shape, F32),
+            pltpu.VMEM((1, head_count), F32),
+            pltpu.VMEM((1, tok), jnp.int32),
+            pltpu.VMEM((head_count, tok), BF16),
             pltpu.VMEM((G, wx, tok), BF16),
             pltpu.VMEM((G, wm, tok), BF16),
             pltpu.VMEM((tok, tok), BF16),
@@ -494,6 +513,7 @@
             pltpu.VMEM((G, states, wx), F32),
             pltpu.VMEM((G, states, wx), F32),
             dma((2, G)),
+            dma((5,)),
             dma((G,)),
             dma((G,)),
             dma((1,)),
@@ -507,8 +527,9 @@
         compiler_params=pltpu.CompilerParams(
             collective_id=0, has_side_effects=True, vmem_limit_bytes=VLIM),
         name="prefill",
-    )(prompt_sizes, skip_gain, log_rates.reshape(1, head_count), packing,
-      inputs, projections, step_sizes)
+    )(*[pltpu.with_memory_space_constraint(part, pltpu.HBM) for part in (
+        prompt_sizes, skip_gain, log_rates.reshape(1, head_count), packing,
+        inputs, projections, step_sizes)])
 
 
 def solution(mesh):

time: 95.7 us -> 92.6 us (0.968)
  Pallas kernels: 92.5 us -> 90.4 us
  local copies, waits for them, and re-layouts: 3.05 us -> 1.32 us
    pallas_call x1, Pallas kernels: 92.5 us -> 90.4 us  [per_device(): pl.pallas_call(functools.partial(fused_kernel, n, heads, width, states, s...]
    unnamed x1, local copies, waits for them, and re-layouts: 3.05 us -> 1.32 us
where the time goes in v4:
time: 92.6 us; the launch traced here: 91.7 us
  Pallas kernels  90.4 us (98%)
  local copies, waits for them, and re-layouts  1.32 us (1%)
    pallas_call x1, Pallas kernels, per_device(): pl.pallas_call(functools.partial(fused_kernel, n, heads, width, states, s...  90.4 us

profile of v4, /device:TPU:26, one launch (start us, length us, event | category | flops | bytes accessed | tf_op | source)
XLA Modules:
  0.0 91.7 jit_solution(12276521315736593087)
XLA Ops:
  0.0 90.4 %prefill.1 = bf16[4096,256]{1,0:T(8,128)(2,1)S(1)} custom-call(s32[4]{0:T(128)} %sizes_hbm.1, f32[64]{0:T(128)} %skip_hbm.1, f32[1,64]{1,0:T(1,128)} %bitcast.1, s32[1,256]{1,0:T(1,128)} %pack_hbm.1, bf16[4096,256]{1,0:T(8,128)(2,1)} %x_hbm.1, bf16[512,256]{1,0:T(8,128)(2,1)} %bc_hbm.1, bf16[64,256]{1,0:T(8,128)(2,1)} %dt_hbm.1), custom_call_target="tpu_custom_call" | custom-call | tf_op jit(solution)/shard_map/prefill/pallas_call | solution.py:483
  90.4 1.3 %copy.9 = bf16[4096,256]{1,0:T(8,128)(2,1)} copy(bf16[4096,256]{1,0:T(8,128)(2,1)S(1)} %prefill.1) | data formatting | bytes 4194304

commit v5 on v4

--- a/solution.py
+++ b/solution.py
@@ -423,10 +423,14 @@
     final = z == nz - 1
     ahead = (z < nz // 2) & jnp.logical_not(final)
 
+    def settle_group(g):
+        carry_stage(g)
+        output_stage(g)
+
     def turn(g):
         @pl.when(ahead & (g == G - 1))
         def _():
-            loop(G - 1, carry_stage)
+            loop(G - 1, settle_group)
 
         loop(n, lambda off: send_y(g, off).wait_recv(), low=1)
         keep_y(g).wait()
@@ -439,7 +443,8 @@
 
             @pl.when(jnp.logical_not(final))
             def _():
-                loop(G, carry_stage, low=jnp.where(ahead, G - 1, 0))
+                loop(G - 1, settle_group, low=jnp.where(ahead, G - 1, 0))
+                carry_stage(G - 1)
 
         inner_stage(g)
 
@@ -455,7 +460,7 @@
             carry_stage(g)
         output_stage(g)
 
-    loop(G, wrap)
+    loop(G, wrap, low=jnp.where(final, 0, G - 1))
     loop(n, lambda off: send_d(off).wait_send(), low=1)
 
     def close(g):

time: 92.6 us -> 92.3 us (level)
  no operation moved by 1% of the time
where the time goes in v5:
time: 92.3 us; the launch traced here: 92.1 us
  Pallas kernels  90.8 us (98%)
  local copies, waits for them, and re-layouts  1.32 us (1%)
    pallas_call x1, Pallas kernels, per_device(): pl.pallas_call(functools.partial(fused_kernel, n, heads, width, states, s...  90.8 us

profile of v5, /device:TPU:26, one launch (start us, length us, event | category | flops | bytes accessed | tf_op | source)
XLA Modules:
  0.0 92.1 jit_solution(11665999957478382460)
XLA Ops:
  0.0 90.8 %prefill.1 = bf16[4096,256]{1,0:T(8,128)(2,1)S(1)} custom-call(s32[4]{0:T(128)} %sizes_hbm.1, f32[64]{0:T(128)} %skip_hbm.1, f32[1,64]{1,0:T(1,128)} %bitcast.1, s32[1,256]{1,0:T(1,128)} %pack_hbm.1, bf16[4096,256]{1,0:T(8,128)(2,1)} %x_hbm.1, bf16[512,256]{1,0:T(8,128)(2,1)} %bc_hbm.1, bf16[64,256]{1,0:T(8,128)(2,1)} %dt_hbm.1), custom_call_target="tpu_custom_call" | custom-call | tf_op jit(solution)/shard_map/prefill/pallas_call | solution.py:488
  90.8 1.3 %copy.9 = bf16[4096,256]{1,0:T(8,128)(2,1)} copy(bf16[4096,256]{1,0:T(8,128)(2,1)S(1)} %prefill.1) | data formatting | bytes 4194304
